TPU v7x, 32 devices: a whole 2x2x4 slice. The times are simulated.
32 devices in a mesh: heads: 4 (over z), rows: 8 (over y, x, core).
Axes of the slice: x: 2, y: 2, z: 4, core: 2. Of those that a mesh axis runs over, the one named last changes fastest.
Arguments:
- tokens: bfloat16 [4, 2048, 1024], P(None, 'rows'), may hold values from -6 to 6
- cam_index: int32 [4, 2048], P(None, 'rows'), may hold values from 0 to 31
- patches: bfloat16 [4, 2048, 768], P(None, 'rows'), may hold values from -6 to 6
- patch_len: int32 [4], replicated, may hold values from 512 to 2048, as said below
- camera_table: bfloat16 [32, 2, 1024], replicated, may hold values from -3 to 3
- self_weights: bfloat16 [3, 1024, 1024], P(None, None, 'heads'), may hold values from -0.1875 to 0.1875
- self_output: bfloat16 [1024, 1024], P('heads'), may hold values from -4 to 4
- cross_gain: bfloat16 [1024], replicated, may hold values from 0.5 to 1.5
- cross_query: bfloat16 [1024, 1024], P(None, 'heads'), may hold values from -0.1875 to 0.1875
- cross_pair: bfloat16 [2, 1024, 1024], P(None, None, 'heads'), may hold values from -0.1875 to 0.1875
- cross_output: bfloat16 [1024, 1024], P('heads'), may hold values from -4 to 4
- patch_weights: bfloat16 [768, 1024], replicated, may hold values from -0.21875 to 0.21875
- hidden_gain: bfloat16 [1024], replicated, may hold values from 0.5 to 1.5
- widen_weights: bfloat16 [1024, 4096], P(None, 'heads'), may hold values from -0.1875 to 0.1875
- narrow_weights: bfloat16 [4096, 1024], P('heads'), may hold values from -0.09375 to 0.09375
- cotangent: bfloat16 [4, 2048, 1024], P(None, 'rows'), may hold values from -6 to 6
Outputs:
- tokens_out: bfloat16 [4, 2048, 1024], P(None, 'rows')
- input_grad: float32 [4, 2048, 1024], P(None, 'rows')
- patch_grad: float32 [4, 2048, 768], P(None, 'rows')
- grad_camera_table: float32 [32, 2, 1024], P(None, None, 'heads')
- grad_self_weights: float32 [3, 1024, 1024], P(None, None, 'heads')
- grad_self_output: float32 [1024, 1024], P('heads')
- grad_cross_gain: float32 [1024], P('heads')
- grad_cross_query: float32 [1024, 1024], P(None, 'heads')
- grad_cross_pair: float32 [2, 1024, 1024], P(None, None, 'heads')
- grad_cross_output: float32 [1024, 1024], P('heads')
- grad_patch_weights: float32 [768, 1024], P(None, 'heads')
- grad_hidden_gain: float32 [1024], P('heads')
- grad_widen_weights: float32 [1024, 4096], P(None, 'heads')
- grad_narrow_weights: float32 [4096, 1024], P('heads')
Inputs may be any that keep to these rules, and one draw needn't show every extreme that they name: `patch_len`: each entry is 2048 or a quarter of 2048; both values occur in every draw. Live patch tokens are the first ones of the object.
All inputs are finite; a program needn't handle non-finite values.
Results may differ from a plain program's by a relative error of at most 0.028.
The roundings to bfloat16 on the way count: a program that leaves them out, or rounds other values in their place, can miss the bound.
Values may be sent and summed in bfloat16 or wider, within the bound.
No kernel may reach another device: no remote copies, remote signals or barrier semaphores. Data moves between devices by JAX's collectives and lax.ppermute only.
A program may use at most 448 MiB of HBM per device.

v0:
```python
from functools import reduce
import jax
import jax.numpy as jnp
from jax import lax
from jax.sharding import PartitionSpec as P

HEAD_DIM = 64
EPSILON = 1e-05


def layer_norm(inputs):
    centred = inputs - jnp.mean(inputs, axis=-1, keepdims=True)
    return centred * lax.rsqrt(jnp.mean(centred * centred, axis=-1, keepdims=True) + EPSILON)


def modulated(inputs, shift_scale):
    return layer_norm(inputs) * (1.0 + shift_scale[:, 0]) + shift_scale[:, 1]


def gained(inputs, gain_row):
    return layer_norm(inputs) * gain_row


def gelu_tanh(pre_act):
    return jax.nn.gelu(pre_act, approximate=True)


def by_heads(matrix):
    return matrix.reshape(matrix.shape[0], -1, HEAD_DIM)


def scaled_scores(queries, key_rows):
    return jnp.einsum(
        "qhe,khe->hqk", queries, key_rows, preferred_element_type=jnp.float32
    ) * HEAD_DIM ** (-0.5)


def attend_forward(queries, key_rows, value_rows, mask_add):
    scores = scaled_scores(queries, key_rows) + mask_add
    row_peak = jnp.max(scores, axis=-1, keepdims=True)
    raised = jnp.exp(scores - row_peak)
    row_total = jnp.sum(raised, axis=-1, keepdims=True)
    attn_probs = (raised / row_total).astype(jnp.bfloat16)
    mixed_out = jnp.einsum(
        "hqk,khe->qhe", attn_probs, value_rows, preferred_element_type=jnp.float32
    )
    return (mixed_out.reshape(mixed_out.shape[0], -1).astype(jnp.bfloat16), row_peak, row_total)


def attend_queries_back(queries, key_rows, value_rows, mask_add, row_peak, row_total, grad_mixed):
    score_scale = HEAD_DIM ** (-0.5)
    scores = scaled_scores(queries, key_rows) + mask_add
    attn_probs = jnp.exp(scores - row_peak) / row_total
    grad_probs = jnp.einsum(
        "qhe,khe->hqk", grad_mixed, value_rows, preferred_element_type=jnp.float32
    )
    spread = jnp.sum(attn_probs * grad_probs, axis=-1, keepdims=True)
    grad_scores = (attn_probs * (grad_probs - spread)).astype(jnp.bfloat16)
    grad_queries = (
        jnp.einsum("hqk,khe->qhe", grad_scores, key_rows, preferred_element_type=jnp.float32)
        * score_scale
    )
    return (grad_queries, spread)


def attend_keys_back(
    all_queries, key_rows, value_rows, mask_add, all_peak, all_total, all_spread, all_grad
):
    score_scale = HEAD_DIM ** (-0.5)
    scores = scaled_scores(all_queries, key_rows) + mask_add
    attn_probs = jnp.exp(scores - all_peak) / all_total
    grad_probs = jnp.einsum(
        "qhe,khe->hqk", all_grad, value_rows, preferred_element_type=jnp.float32
    )
    grad_scores = (attn_probs * (grad_probs - all_spread)).astype(jnp.bfloat16)
    grad_keys = (
        jnp.einsum("hqk,qhe->khe", grad_scores, all_queries, preferred_element_type=jnp.float32)
        * score_scale
    )
    grad_values = jnp.einsum(
        "hqk,qhe->khe",
        attn_probs.astype(jnp.bfloat16),
        all_grad,
        preferred_element_type=jnp.float32,
    )
    return (grad_keys, grad_values)


def owner_key_grads(
    queries, grad_mixed, row_peak, row_total, spread, own_keys, own_values, own_mask
):
    gathered_queries, gathered_grads = (
        lax.all_gather(queries, "rows", axis=0, tiled=True),
        lax.all_gather(grad_mixed, "rows", axis=0, tiled=True),
    )
    gathered_peak, gathered_total, gathered_spread = (
        lax.all_gather(row_peak[:, :, 0].T, "rows", axis=0, tiled=True),
        lax.all_gather(row_total[:, :, 0].T, "rows", axis=0, tiled=True),
        lax.all_gather(spread[:, :, 0].T, "rows", axis=0, tiled=True),
    )
    grad_keys, grad_values = attend_keys_back(
        by_heads(gathered_queries),
        by_heads(own_keys),
        by_heads(own_values),
        own_mask,
        gathered_peak.T[:, :, None],
        gathered_total.T[:, :, None],
        gathered_spread.T[:, :, None],
        by_heads(gathered_grads),
    )
    return (grad_keys.reshape(own_keys.shape[0], -1), grad_values.reshape(own_keys.shape[0], -1))


def add_trees(former, latter):
    return jax.tree.map(jnp.add, former, latter)


def per_device(
    tokens,
    cam_index,
    patches,
    patch_len,
    camera_table,
    self_weights,
    self_output,
    cross_gain,
    cross_query,
    cross_pair,
    cross_output,
    patch_weights,
    hidden_gain,
    widen_weights,
    narrow_weights,
    cotangent,
):
    batches = tokens.shape[0]
    row_count = tokens.shape[1]
    model_width = tokens.shape[2]
    local_cols = self_weights.shape[2]
    code_count = camera_table.shape[0]
    patch_rows = patches.shape[1]
    row_rank = lax.axis_index("rows")
    head_rank = lax.axis_index("heads")
    all_patches = patch_rows * lax.axis_size("rows")
    table_flat = camera_table.reshape(code_count, -1).astype(jnp.float32)
    patch_index = jnp.arange(all_patches)
    own_index = row_rank * patch_rows + jnp.arange(patch_rows)
    cross_gain_f = cross_gain.astype(jnp.float32)
    hidden_gain_f = hidden_gain.astype(jnp.float32)
    outputs = []
    input_grads = []
    patch_grads = []
    contributions = []
    for microbatch in range(batches):
        inputs = tokens[microbatch].astype(jnp.float32)
        onehot = (cam_index[microbatch][:, None] == jnp.arange(code_count)[None, :]).astype(
            jnp.float32
        )
        shift_scale = jnp.dot(onehot, table_flat, precision=lax.Precision.HIGHEST).reshape(
            row_count, 2, model_width
        )
        normed_one, norm_one_back = jax.vjp(modulated, inputs, shift_scale)
        normed_one_low = normed_one.astype(jnp.bfloat16)
        projected = jnp.einsum(
            "rd,tdc->trc", normed_one_low, self_weights, preferred_element_type=jnp.float32
        ).astype(jnp.bfloat16)
        queries = projected[0]
        all_keys, all_values = (
            lax.all_gather(projected[1], "rows", axis=0, tiled=True),
            lax.all_gather(projected[2], "rows", axis=0, tiled=True),
        )
        self_mixed, self_peak, self_total = attend_forward(
            by_heads(queries), by_heads(all_keys), by_heads(all_values), 0.0
        )
        attn_sum = lax.psum(
            jnp.dot(self_mixed, self_output, preferred_element_type=jnp.float32), "heads"
        )
        after_self = inputs + attn_sum
        normed_two, norm_two_back = jax.vjp(gained, after_self, cross_gain_f)
        normed_two_low = normed_two.astype(jnp.bfloat16)
        cross_queries = jnp.dot(
            normed_two_low, cross_query, preferred_element_type=jnp.float32
        ).astype(jnp.bfloat16)
        patch_mid = jnp.dot(
            patches[microbatch], patch_weights, preferred_element_type=jnp.float32
        ).astype(jnp.bfloat16)
        patch_pair = jnp.einsum(
            "pd,tdc->tpc", patch_mid, cross_pair, preferred_element_type=jnp.float32
        ).astype(jnp.bfloat16)
        own_keys = patch_pair[0]
        own_values = patch_pair[1]
        cross_keys_all, cross_values_all = (
            lax.all_gather(own_keys, "rows", axis=0, tiled=True),
            lax.all_gather(own_values, "rows", axis=0, tiled=True),
        )
        mask_add = jnp.where(patch_index < patch_len[microbatch], 0.0, -1e30).astype(jnp.float32)
        cross_mixed, cross_peak, cross_total = attend_forward(
            by_heads(cross_queries), by_heads(cross_keys_all), by_heads(cross_values_all), mask_add
        )
        cross_sum = lax.psum(
            jnp.dot(cross_mixed, cross_output, preferred_element_type=jnp.float32).astype(
                jnp.bfloat16
            ),
            "heads",
        ).astype(jnp.float32)
        after_cross = after_self + cross_sum
        normed_three, norm_three_back = jax.vjp(gained, after_cross, hidden_gain_f)
        normed_three_low = normed_three.astype(jnp.bfloat16)
        pre_act = jnp.dot(normed_three_low, widen_weights, preferred_element_type=jnp.float32)
        activated, act_back = jax.vjp(gelu_tanh, pre_act)
        activated_low = activated.astype(jnp.bfloat16)
        hidden_sum = lax.psum(
            jnp.dot(activated_low, narrow_weights, preferred_element_type=jnp.float32).astype(
                jnp.bfloat16
            ),
            "heads",
        ).astype(jnp.float32)
        outputs.append((after_cross + hidden_sum).astype(jnp.bfloat16))
        grad_low = cotangent[microbatch]
        grad_top = grad_low.astype(jnp.float32)
        narrow_term = jnp.einsum(
            "rf,rd->fd", activated_low, grad_low, preferred_element_type=jnp.float32
        )
        grad_act = jnp.einsum(
            "rd,fd->rf", grad_low, narrow_weights, preferred_element_type=jnp.float32
        )
        grad_pre = act_back(grad_act)[0].astype(jnp.bfloat16)
        widen_term = jnp.einsum(
            "rd,rf->df", normed_three_low, grad_pre, preferred_element_type=jnp.float32
        )
        grad_normed_three = lax.psum(
            jnp.einsum(
                "rf,df->rd", grad_pre, widen_weights, preferred_element_type=jnp.float32
            ).astype(jnp.bfloat16),
            "heads",
        ).astype(jnp.float32)
        grad_mid, hidden_gain_term = norm_three_back(grad_normed_three)
        grad_cross = grad_top + grad_mid
        grad_cross_low = grad_cross.astype(jnp.bfloat16)
        cross_output_term = jnp.einsum(
            "rc,rd->cd", cross_mixed, grad_cross_low, preferred_element_type=jnp.float32
        )
        grad_cross_mixed = jnp.einsum(
            "rd,cd->rc", grad_cross_low, cross_output, preferred_element_type=jnp.float32
        ).astype(jnp.bfloat16)
        grad_cq, cross_spread = attend_queries_back(
            by_heads(cross_queries),
            by_heads(cross_keys_all),
            by_heads(cross_values_all),
            mask_add,
            cross_peak,
            cross_total,
            by_heads(grad_cross_mixed),
        )
        own_mask = jnp.where(own_index < patch_len[microbatch], 0.0, -1e30).astype(jnp.float32)
        grad_ck, grad_cv = owner_key_grads(
            cross_queries,
            grad_cross_mixed,
            cross_peak,
            cross_total,
            cross_spread,
            own_keys,
            own_values,
            own_mask,
        )
        grad_pair_low = jnp.stack([grad_ck, grad_cv]).astype(jnp.bfloat16)
        pair_term = jnp.einsum(
            "pd,tpc->tdc", patch_mid, grad_pair_low, preferred_element_type=jnp.float32
        )
        grad_cq_low = grad_cq.reshape(row_count, -1).astype(jnp.bfloat16)
        query_term = jnp.einsum(
            "rd,rc->dc", normed_two_low, grad_cq_low, preferred_element_type=jnp.float32
        )
        grad_normed_two, grad_patch_mid = (
            lax.psum(
                jnp.einsum(
                    "rc,dc->rd", grad_cq_low, cross_query, preferred_element_type=jnp.float32
                ).astype(jnp.bfloat16),
                "heads",
            ).astype(jnp.float32),
            lax.psum(
                jnp.einsum(
                    "tpc,tdc->pd", grad_pair_low, cross_pair, preferred_element_type=jnp.float32
                ).astype(jnp.bfloat16),
                "heads",
            ).astype(jnp.float32),
        )
        grad_mid_low = grad_patch_mid.astype(jnp.bfloat16)
        own_columns = lax.dynamic_slice_in_dim(grad_mid_low, head_rank * local_cols, local_cols, 1)
        patch_term = jnp.einsum(
            "pe,pc->ec", patches[microbatch], own_columns, preferred_element_type=jnp.float32
        )
        patch_grads.append(
            jnp.einsum("pd,ed->pe", grad_mid_low, patch_weights, preferred_element_type=jnp.float32)
        )
        grad_after_self, cross_gain_term = norm_two_back(grad_normed_two)
        grad_self = grad_cross + grad_after_self
        grad_self_low = grad_self.astype(jnp.bfloat16)
        self_output_term = jnp.einsum(
            "rc,rd->cd", self_mixed, grad_self_low, preferred_element_type=jnp.float32
        )
        grad_self_mixed = jnp.einsum(
            "rd,cd->rc", grad_self_low, self_output, preferred_element_type=jnp.float32
        ).astype(jnp.bfloat16)
        grad_q, self_spread = attend_queries_back(
            by_heads(queries),
            by_heads(all_keys),
            by_heads(all_values),
            0.0,
            self_peak,
            self_total,
            by_heads(grad_self_mixed),
        )
        grad_k, grad_v = owner_key_grads(
            queries,
            grad_self_mixed,
            self_peak,
            self_total,
            self_spread,
            projected[1],
            projected[2],
            0.0,
        )
        grad_proj = jnp.stack([grad_q.reshape(row_count, -1), grad_k, grad_v]).astype(jnp.bfloat16)
        self_term = jnp.einsum(
            "rd,trc->tdc", normed_one_low, grad_proj, preferred_element_type=jnp.float32
        )
        grad_normed_one = lax.psum(
            jnp.einsum(
                "trc,tdc->rd", grad_proj, self_weights, preferred_element_type=jnp.float32
            ).astype(jnp.bfloat16),
            "heads",
        ).astype(jnp.float32)
        grad_inputs, grad_shift_scale = norm_one_back(grad_normed_one)
        table_term = jnp.dot(
            onehot.T, grad_shift_scale.reshape(row_count, -1), precision=lax.Precision.HIGHEST
        )
        input_grads.append(grad_self + grad_inputs)
        contributions.append(
            (
                table_term,
                self_term,
                self_output_term,
                cross_gain_term,
                query_term,
                pair_term,
                cross_output_term,
                patch_term,
                hidden_gain_term,
                widen_term,
                narrow_term,
            )
        )
    summed = reduce(add_trees, contributions)
    table_part = lax.dynamic_slice_in_dim(
        summed[0].reshape(code_count, 2, model_width), head_rank * local_cols, local_cols, 2
    )
    cross_gain_part = lax.dynamic_slice_in_dim(summed[3], head_rank * local_cols, local_cols, 0)
    hidden_gain_part = lax.dynamic_slice_in_dim(summed[8], head_rank * local_cols, local_cols, 0)
    totals = (
        lax.psum(table_part.astype(jnp.bfloat16), "rows").astype(jnp.float32),
        lax.psum(summed[1].astype(jnp.bfloat16), "rows").astype(jnp.float32),
        lax.psum(summed[2].astype(jnp.bfloat16), "rows").astype(jnp.float32),
        lax.psum(cross_gain_part.astype(jnp.bfloat16), "rows").astype(jnp.float32),
        lax.psum(summed[4].astype(jnp.bfloat16), "rows").astype(jnp.float32),
        lax.psum(summed[5].astype(jnp.bfloat16), "rows").astype(jnp.float32),
        lax.psum(summed[6].astype(jnp.bfloat16), "rows").astype(jnp.float32),
        lax.psum(summed[7].astype(jnp.bfloat16), "rows").astype(jnp.float32),
        lax.psum(hidden_gain_part.astype(jnp.bfloat16), "rows").astype(jnp.float32),
        lax.psum(summed[9].astype(jnp.bfloat16), "rows").astype(jnp.float32),
        lax.psum(summed[10].astype(jnp.bfloat16), "rows").astype(jnp.float32),
    )
    return (jnp.stack(outputs), jnp.stack(input_grads), jnp.stack(patch_grads)) + tuple(totals)


def solution(mesh):
    in_specs = (
        P(None, "rows", None),
        P(None, "rows"),
        P(None, "rows", None),
        P(),
        P(),
        P(None, None, "heads"),
        P("heads", None),
        P(),
        P(None, "heads"),
        P(None, None, "heads"),
        P("heads", None),
        P(),
        P(),
        P(None, "heads"),
        P("heads", None),
        P(None, "rows", None),
    )
    out_specs = (
        P(None, "rows", None),
        P(None, "rows", None),
        P(None, "rows", None),
        P(None, None, "heads"),
        P(None, None, "heads"),
        P("heads", None),
        P("heads"),
        P(None, "heads"),
        P(None, None, "heads"),
        P("heads", None),
        P(None, "heads"),
        P("heads"),
        P(None, "heads"),
        P("heads", None),
    )
    return jax.shard_map(
        per_device, mesh=mesh, in_specs=in_specs, out_specs=out_specs, check_vma=False
    )
```

profile of v0, /device:TPU:0, one launch (start us, length us, event | category | flops | bytes accessed | tf_op | source)
XLA Modules:
  0.0 1912.5 jit_solution(12267981073876656317)
XLA Ops:
  36.8 9.2 all-gather.87.cloned.1.call-done
  53.8 17.8 all-gather.85.cloned.1.call-done
  78.5 19.1 all-gather.103.cloned.1.call-done
  105.1 17.8 all-gather.101.cloned.1.call-done
  128.6 20.3 %all-gather.95.cloned.1.call-done = bf16[1,2048,256]{1,2,0:T(8,128)(2,1)} async-done(((bf16[1,256,256]{1,2,0:T(8,128)(2,1)}), bf16[1,2048,256]{1,2,0:T(8,128)(2,1)}) %all-gather.95.cloned.1.call-update) | async-done | bytes 1048592 | tf_op jit(solution)/shard_map/all_gather | solution.py:169
  156.3 17.9 all-gather.93.cloned.1.call-done
  179.8 19.8 %all-gather.79.cloned.1.call-done = bf16[1,2048,256]{1,2,0:T(8,128)(2,1)} async-done(((bf16[1,256,256]{1,2,0:T(8,128)(2,1)}), bf16[1,2048,256]{1,2,0:T(8,128)(2,1)}) %all-gather.79.cloned.1.call-update) | async-done | bytes 1048592 | tf_op jit(solution)/shard_map/all_gather | solution.py:169
  210.0 15.2 all-gather.77.cloned.1.call-done
  262.0 9.0 all_gather.196
  271.0 8.1 all_gather.195
  279.1 9.0 all_gather.191
  296.2 9.0 all_gather.186
  331.8 9.1 all_gather.201
  349.1 112.7 %all-reduce.22.cloned.1.call-done = (f32[256,1024]{1,0:T(8,128)}, f32[256,1024]{1,0:T(8,128)}, f32[256,1024]{1,0:T(8,128)}, f32[256,1024]{1,0:T(8,128)}) async-done(((f32[256,1024]{1,0:T(8,128)}, f32[256,1024]{1,0:T(8,128)}, f32[256,1024]{1,0:T(8,128)}, f32[256,1024]{1,0:T(8,128)}), (f32[256,1024]{1,0:T(8,128)}, f32[256,1024]{1,0:T(8,128)}, f32[256,1024]{1,0:T(8,128)}, ...) | async-done | bytes 4194320 | tf_op jit(solution)/shard_map/psum | solution.py:175
  469.0 17.5 all-gather.115.cloned.1.call-done
  494.1 17.8 all-gather.107.cloned.1.call-done
  516.7 10.0 all_gather.221
  526.7 9.1 all_gather.220
  547.5 15.5 all-gather.89.cloned.1.call-done
  568.9 19.6 %all-gather.83.cloned.1.call-done = bf16[1,2048,256]{1,2,0:T(8,128)(2,1)} async-done(((bf16[1,256,256]{1,2,0:T(8,128)(2,1)}), bf16[1,2048,256]{1,2,0:T(8,128)(2,1)}) %all-gather.83.cloned.1.call-update) | async-done | bytes 1048592 | tf_op jit(solution)/shard_map/all_gather | solution.py:193
  596.9 17.1 all-gather.81.cloned.1.call-done
  619.9 19.8 %all-gather.99.cloned.1.call-done = bf16[1,2048,256]{1,2,0:T(8,128)(2,1)} async-done(((bf16[1,256,256]{1,2,0:T(8,128)(2,1)}), bf16[1,2048,256]{1,2,0:T(8,128)(2,1)}) %all-gather.99.cloned.1.call-update) | async-done | bytes 1048592 | tf_op jit(solution)/shard_map/all_gather | solution.py:193
  647.5 10.0 all_gather.216
  657.5 9.1 all_gather.215
  666.6 10.4 all_gather.211
  685.1 9.1 all_gather.210
  694.2 9.9 all_gather.206
  704.2 9.1 all_gather.205
  729.4 12.9 all-gather.69.cloned.1.call-done
  748.4 19.4 %all-gather.65.cloned.1.call-done = bf16[2048,256]{0,1:T(8,128)(2,1)} async-done(((bf16[256,256]{0,1:T(8,128)(2,1)}), bf16[2048,256]{0,1:T(8,128)(2,1)}) %all-gather.65.cloned.1.call-update) | async-done | bytes 1048592 | tf_op jit(solution)/shard_map/all_gather | solution.py:93
  774.0 19.4 %all-gather.61.cloned.1.call-done = bf16[2048,256]{0,1:T(8,128)(2,1)} async-done(((bf16[256,256]{0,1:T(8,128)(2,1)}), bf16[2048,256]{0,1:T(8,128)(2,1)}) %all-gather.61.cloned.1.call-update) | async-done | bytes 1048592 | tf_op jit(solution)/shard_map/all_gather | solution.py:93
  799.6 85.7 %all-reduce.32.cloned.1.call-done = (bf16[256,1024]{1,0:T(8,128)(2,1)}, bf16[256,1024]{1,0:T(8,128)(2,1)}, bf16[256,1024]{1,0:T(8,128)(2,1)}, bf16[256,1024]{1,0:T(8,128)(2,1)}) async-done(((bf16[256,1024]{1,0:T(8,128)(2,1)}, bf16[256,1024]{1,0:T(8,128)(2,1)}, bf16[256,1024]{1,0:T(8,128)(2,1)}, bf16[256,1024]{1,0:T(8,128)(2,1)}), (bf16[256,1024]{1,0:T(8,128)(2,1)}, bf16[256,1024]{1,0:T(8,128)(2,1)}, ...) | async-done | bytes 2097168 | tf_op jit(solution)/shard_map/psum | solution.py:200
  940.0 68.7 %all-reduce.30.cloned.1.call-done = (bf16[256,1024]{1,0:T(8,128)(2,1)}, bf16[256,1024]{1,0:T(8,128)(2,1)}, bf16[256,1024]{1,0:T(8,128)(2,1)}, bf16[256,1024]{1,0:T(8,128)(2,1)}) async-done(((bf16[256,1024]{1,0:T(8,128)(2,1)}, bf16[256,1024]{1,0:T(8,128)(2,1)}, bf16[256,1024]{1,0:T(8,128)(2,1)}, bf16[256,1024]{1,0:T(8,128)(2,1)}), (bf16[256,1024]{1,0:T(8,128)(2,1)}, bf16[256,1024]{1,0:T(8,128)(2,1)}, ...) | async-done | bytes 2097168 | tf_op jit(solution)/shard_map/psum | solution.py:231
  1042.3 9.0 all_gather.223
  1051.4 9.0 all_gather.218
  1076.5 8.3 all_gather.213
  1093.7 9.0 all_gather.208
  1179.4 61.4 %all-reduce.28.cloned.1.call-done = (bf16[256,1024]{1,0:T(8,128)(2,1)}, bf16[256,1024]{1,0:T(8,128)(2,1)}, bf16[256,1024]{1,0:T(8,128)(2,1)}, bf16[256,1024]{1,0:T(8,128)(2,1)}) async-done(((bf16[256,1024]{1,0:T(8,128)(2,1)}, bf16[256,1024]{1,0:T(8,128)(2,1)}, bf16[256,1024]{1,0:T(8,128)(2,1)}, bf16[256,1024]{1,0:T(8,128)(2,1)}), (bf16[256,1024]{1,0:T(8,128)(2,1)}, bf16[256,1024]{1,0:T(8,128)(2,1)}, ...) | async-done | bytes 2097168 | tf_op jit(solution)/shard_map/psum | solution.py:275
  1272.3 10.3 multiply_reduce_fusion.4
  1293.0 9.3 fusion.176
  1326.3 8.5 fusion.178
  1335.6 10.7 all_gather.198
  1346.3 9.3 all_gather.193
  1355.6 10.2 all_gather.188
  1365.8 9.3 all_gather.203
  1471.0 204.0 %all-reduce.26.cloned.1.call-done = (bf16[256,1024]{1,0:T(8,128)(2,1)}, bf16[256,1024]{1,0:T(8,128)(2,1)}, bf16[256,1024]{1,0:T(8,128)(2,1)}, bf16[256,1024]{1,0...) async-done(((bf16[256,1024]{1,0:T(8,128)(2,1)}, ...) | async-done | bytes 6291472 | tf_op jit(solution)/shard_map/psum | solution.py:281
  1722.2 24.8 %all-reduce.9 = (bf16[32,2,256]{2,1,0:T(2,128)(2,1)S(1)}, bf16[256]{0:T(256)(128)(2,1)S(1)}, bf16[256]{0:T(256)(128)(2,1)S(1)}) all-reduce(bf16[32,2,256]{2,1,0:T(2,128)(2,1)S(1)} %dynamic-slice_convert_fusion, bf16[256]{0:T(256)(128)(2,1)S(1)} %dynamic_slice.40, ...), channel_id=1, replica_groups=mesh['heads'=4,'rows'=8] {'rows'}, use_global_device_ids=true, to_apply=%region_100.101 | all-reduce | flops 16896 | bytes 67584 | tf_op jit(solution)/shard_map/psum | solution.py:361
  1769.1 116.2 %all-reduce.24.cloned.1.call-done = (bf16[3,1024,256]{1,2,0:T(8,128)(2,1)}, bf16[2,1024,256]{1,2,0:T(8,128)(2,1)}, bf16[768,256]{0,1:T(8,128)(2,1)}, bf16[256,10...) async-done(((bf16[3,1024,256]{1,2,0:T(8,128)(2,1)}, ...) | async-done | bytes 8781840 | tf_op jit(solution)/shard_map/psum | solution.py:362
  (1086 shorter events, 700.1 us)
Async XLA Ops:
  7.2 880.9 %copy-start = (bf16[1024,1024]{1,0:T(8,128)(2,1)S(1)}, bf16[1024,1024]{1,0:T(8,128)(2,1)}, u32[]{:S(2)}) copy-start(bf16[1024,1024]{1,0:T(8,128)(2,1)} %param.29) | copy-start | bytes 6291460
  7.2 38.8 %all-gather.87.cloned.1.call-start = ((), (), s32[]{:S(2)}) async-start(), calls=%async_computation.17 | async-start | bytes 1179648 | tf_op jit(solution)/shard_map/all_gather | solution.py:169
  19.6 51.9 %all-gather.85.cloned.1.call-start = ((), (), s32[]{:S(2)}) async-start(), calls=%async_computation.16 | async-start | bytes 1179648 | tf_op jit(solution)/shard_map/all_gather | solution.py:170
  20.4 77.2 %all-gather.103.cloned.1.call-start = ((), (), s32[]{:S(2)}) async-start(), calls=%async_computation.25 | async-start | bytes 1179648 | tf_op jit(solution)/shard_map/all_gather | solution.py:169
  23.4 99.6 %all-gather.101.cloned.1.call-start = ((), (), s32[]{:S(2)}) async-start(), calls=%async_computation.24 | async-start | bytes 1179648 | tf_op jit(solution)/shard_map/all_gather | solution.py:170
  24.0 124.9 %all-gather.95.cloned.1.call-start = ((), (), s32[]{:S(2)}) async-start(), calls=%async_computation.21 | async-start | bytes 1179648 | tf_op jit(solution)/shard_map/all_gather | solution.py:169
  26.9 147.3 %all-gather.93.cloned.1.call-start = ((), (), s32[]{:S(2)}) async-start(), calls=%async_computation.20 | async-start | bytes 1179648 | tf_op jit(solution)/shard_map/all_gather | solution.py:170
  27.5 172.2 %all-gather.79.cloned.1.call-start = ((), (), s32[]{:S(2)}) async-start(), calls=%async_computation.13 | async-start | bytes 1179648 | tf_op jit(solution)/shard_map/all_gather | solution.py:169
  34.0 191.2 %all-gather.77.cloned.1.call-start = ((), (), s32[]{:S(2)}) async-start(), calls=%async_computation.12 | async-start | bytes 1179648 | tf_op jit(solution)/shard_map/all_gather | solution.py:170
  34.7 278.7 %all-gather.113.cloned.1.call-start = ((), (), s32[]{:S(2)}) async-start(), calls=%async_computation.30 | async-start | bytes 1179648 | tf_op jit(solution)/shard_map/all_gather | solution.py:93
  35.4 284.3 %all-gather.111.cloned.1.call-start = ((), (), s32[]{:S(2)}) async-start(), calls=%async_computation.29 | async-start | bytes 1179648 | tf_op jit(solution)/shard_map/all_gather | solution.py:93
  36.0 289.8 %all-gather.109.cloned.1.call-start = ((), (), s32[]{:S(2)}) async-start(), calls=%async_computation.28 | async-start | bytes 1179648 | tf_op jit(solution)/shard_map/all_gather | solution.py:93
  36.8 425.0 %all-reduce.22.cloned.1.call-start = ((), (), s32[]{:S(2)}) async-start(), calls=%async_computation.32 | async-start | bytes 8388608 | tf_op jit(solution)/shard_map/psum | solution.py:175
  53.8 225.4 %copy-start.262 = (f32[4,256]{1,0:T(4,128)}, f32[4,256]{1,0:T(4,128)S(1)}, u32[]{:S(2)}) copy-start(f32[4,256]{1,0:T(4,128)S(1)} %fusion.7) | copy-start | bytes 12292
  100.2 240.8 %copy-start.224 = (f32[4,256]{1,0:T(4,128)}, f32[4,256]{1,0:T(4,128)S(1)}, u32[]{:S(2)}) copy-start(f32[4,256]{1,0:T(4,128)S(1)} %get-tuple-element.215) | copy-start | bytes 12292
  105.1 226.7 %copy-start.260 = (f32[4,256]{1,0:T(4,128)}, f32[4,256]{1,0:T(4,128)S(1)}, u32[]{:S(2)}) copy-start(f32[4,256]{1,0:T(4,128)S(1)} %fusion.11) | copy-start | bytes 12292
  232.8 253.7 %all-gather.115.cloned.1.call-start = ((), (), s32[]{:S(2)}) async-start(), calls=%async_computation.31 | async-start | bytes 1179648 | tf_op jit(solution)/shard_map/all_gather | solution.py:93
  233.5 278.5 %all-gather.107.cloned.1.call-start = ((), (), s32[]{:S(2)}) async-start(), calls=%async_computation.27 | async-start | bytes 1179648 | tf_op jit(solution)/shard_map/all_gather | solution.py:193
  237.9 301.8 %all-gather.91.cloned.1.call-start = ((), (), s32[]{:S(2)}) async-start(), calls=%async_computation.19 | async-start | bytes 1179648 | tf_op jit(solution)/shard_map/all_gather | solution.py:193
  242.2 320.9 %all-gather.89.cloned.1.call-start = ((), (), s32[]{:S(2)}) async-start(), calls=%async_computation.18 | async-start | bytes 1179648 | tf_op jit(solution)/shard_map/all_gather | solution.py:194
  242.8 345.8 %all-gather.83.cloned.1.call-start = ((), (), s32[]{:S(2)}) async-start(), calls=%async_computation.15 | async-start | bytes 1179648 | tf_op jit(solution)/shard_map/all_gather | solution.py:193
  247.0 367.0 %all-gather.81.cloned.1.call-start = ((), (), s32[]{:S(2)}) async-start(), calls=%async_computation.14 | async-start | bytes 1179648 | tf_op jit(solution)/shard_map/all_gather | solution.py:194
  247.6 392.0 %all-gather.99.cloned.1.call-start = ((), (), s32[]{:S(2)}) async-start(), calls=%async_computation.23 | async-start | bytes 1179648 | tf_op jit(solution)/shard_map/all_gather | solution.py:193
  251.3 427.8 %all-gather.105.cloned.1.call-start = ((), (), s32[]{:S(2)}) async-start(), calls=%async_computation.26 | async-start | bytes 1179648 | tf_op jit(solution)/shard_map/all_gather | solution.py:194
  251.9 463.5 %all-gather.97.cloned.1.call-start = ((), (), s32[]{:S(2)}) async-start(), calls=%async_computation.22 | async-start | bytes 1179648 | tf_op jit(solution)/shard_map/all_gather | solution.py:194
  252.7 470.6 %all-gather.73.cloned.1.call-start = ((), (), s32[]{:S(2)}) async-start(), calls=%async_computation.10 | async-start | bytes 1179648 | tf_op jit(solution)/shard_map/all_gather | solution.py:93
  257.7 284.6 %copy-start.215 = (f32[2048]{0:T(1024)}, f32[2048]{0:T(1024)S(1)}, u32[]{:S(2)}) copy-start(f32[2048]{0:T(1024)S(1)} %fusion.404) | copy-start | bytes 24580
  261.4 276.2 %copy-start.155 = (f32[1024]{0:T(1024)}, f32[1024]{0:T(1024)S(1)}, u32[]{:S(2)}) copy-start(f32[1024]{0:T(1024)S(1)} %convert_element_type.678) | copy-start | bytes 12292
  466.4 431.6 %copy-start.7 = (f32[256,1024]{1,0:T(8,128)}, f32[256,1024]{1,0:T(8,128)S(1)}, u32[]{:S(2)}) copy-start(f32[256,1024]{1,0:T(8,128)S(1)} %get-tuple-element.167) | copy-start | bytes 3145732
  468.9 273.4 %all-gather.69.cloned.1.call-start = ((), (), s32[]{:S(2)}) async-start(), calls=%async_computation.8 | async-start | bytes 1179648 | tf_op jit(solution)/shard_map/all_gather | solution.py:93
  494.1 273.7 %all-gather.65.cloned.1.call-start = ((), (), s32[]{:S(2)}) async-start(), calls=%async_computation.6 | async-start | bytes 1179648 | tf_op jit(solution)/shard_map/all_gather | solution.py:93
  539.4 254.0 %all-gather.61.cloned.1.call-start = ((), (), s32[]{:S(2)}) async-start(), calls=%async_computation.4 | async-start | bytes 1179648 | tf_op jit(solution)/shard_map/all_gather | solution.py:93
  685.1 200.2 %all-reduce.32.cloned.1.call-start = ((), (), s32[]{:S(2)}) async-start(), calls=%async_computation.37 | async-start | bytes 4194304 | tf_op jit(solution)/shard_map/psum | solution.py:200
  723.2 285.5 %all-reduce.30.cloned.1.call-start = ((), (), s32[]{:S(2)}) async-start(), calls=%async_computation.36 | async-start | bytes 4194304 | tf_op jit(solution)/shard_map/psum | solution.py:231
  921.5 200.4 %all-gather.75.cloned.1.call-start = ((), (), s32[]{:S(2)}) async-start(), calls=%async_computation.11 | async-start | bytes 1179648 | tf_op jit(solution)/shard_map/all_gather | solution.py:94
  1035.0 97.8 %all-gather.71.cloned.1.call-start = ((), (), s32[]{:S(2)}) async-start(), calls=%async_computation.9 | async-start | bytes 1179648 | tf_op jit(solution)/shard_map/all_gather | solution.py:94
  1076.4 67.8 %all-gather.67.cloned.1.call-start = ((), (), s32[]{:S(2)}) async-start(), calls=%async_computation.7 | async-start | bytes 1179648 | tf_op jit(solution)/shard_map/all_gather | solution.py:94
  1093.7 62.6 %all-gather.63.cloned.1.call-start = ((), (), s32[]{:S(2)}) async-start(), calls=%async_computation.5 | async-start | bytes 1179648 | tf_op jit(solution)/shard_map/all_gather | solution.py:94
  1111.5 129.3 %all-reduce.28.cloned.1.call-start = ((), (), s32[]{:S(2)}) async-start(), calls=%async_computation.35 | async-start | bytes 4194304 | tf_op jit(solution)/shard_map/psum | solution.py:275
  1121.9 253.6 %all-gather.57.cloned.1.call-start = ((), (), s32[]{:S(2)}) async-start(), calls=%async_computation.2 | async-start | bytes 1179648 | tf_op jit(solution)/shard_map/all_gather | solution.py:94
  1258.2 132.9 %all-gather.55.cloned.1.call-start = ((), (), s32[]{:S(2)}) async-start(), calls=%async_computation.1 | async-start | bytes 1179648 | tf_op jit(solution)/shard_map/all_gather | solution.py:94
  1272.2 134.5 %all-gather.53.cloned.1.call-start = ((), (), s32[]{:S(2)}) async-start(), calls=%async_computation | async-start | bytes 1179648 | tf_op jit(solution)/shard_map/all_gather | solution.py:94
  1291.0 131.4 %all-gather.59.cloned.1.call-start = ((), (), s32[]{:S(2)}) async-start(), calls=%async_computation.3 | async-start | bytes 1179648 | tf_op jit(solution)/shard_map/all_gather | solution.py:94
  1375.2 299.8 %all-reduce.26.cloned.1.call-start = ((), (), s32[]{:S(2)}) async-start(), calls=%async_computation.34 | async-start | bytes 12582912 | tf_op jit(solution)/shard_map/psum | solution.py:281
  1449.2 436.1 %all-reduce.24.cloned.1.call-start = ((), (), s32[]{:S(2)}) async-start(), calls=%async_computation.33 | async-start | bytes 17563648 | tf_op jit(solution)/shard_map/psum | solution.py:362
  1471.0 217.4 %copy-start.303 = (f32[256]{0:T(256)S(1)}, f32[256]{0:T(256)}, u32[]{:S(2)}) copy-start(f32[256]{0:T(256)} %copy-done.302) | copy-start | bytes 3076
  1471.0 217.5 %copy-start.285 = (f32[256]{0:T(256)S(1)}, f32[256]{0:T(256)}, u32[]{:S(2)}) copy-start(f32[256]{0:T(256)} %copy-done.284) | copy-start | bytes 3076
  1471.0 217.5 %copy-start.287 = (f32[256]{0:T(256)S(1)}, f32[256]{0:T(256)}, u32[]{:S(2)}) copy-start(f32[256]{0:T(256)} %copy-done.286) | copy-start | bytes 3076
  (325 other events, 6481.9 us)
Sparse Core Ops, SparseCore 0:
  19.8 26.2 all-gather.86
  47.9 23.5 all-gather.84
  74.0 23.5 all-gather.102
  99.3 23.5 all-gather.100
  125.2 23.5 all-gather.94
  150.6 23.5 all-gather.92
  176.1 23.5 all-gather.78
  201.5 23.5 all-gather.76
  227.6 23.5 all-gather.112
  252.9 23.6 all-gather.110
  278.5 23.6 all-gather.108
  305.7 156.0 all-reduce.21
  463.8 22.6 all-gather.114
  488.4 23.5 all-gather.106
  513.9 23.6 all-gather.90
  539.4 23.5 all-gather.88
  564.9 23.5 all-gather.82
  590.4 23.5 all-gather.80
  616.0 23.5 all-gather.98
  641.5 23.7 all-gather.104
  667.3 23.5 all-gather.96
  693.0 23.6 all-gather.72
  718.7 23.5 all-gather.68
  744.2 23.5 all-gather.64
  769.8 23.5 all-gather.60
  797.2 88.0 all-reduce.31
  921.6 86.9 all-reduce.29
  1035.1 22.6 all-gather.74
  1076.5 21.6 all-gather.70
  1100.1 23.6 all-gather.66
  1126.3 23.5 all-gather.62
  1152.7 87.9 all-reduce.27
  1258.3 22.4 all-gather.56
  1282.7 23.5 all-gather.54
  1308.8 23.6 all-gather.52
  1375.3 22.0 all-gather.58
  1449.3 225.6 all-reduce.25
  1754.9 130.3 all-reduce.23
where the time goes:
time: 1920 us; the launch traced here: 1910 us
  waiting for transfers between devices  953 us (50%)
  matrix products  489 us (25%)
  blocking collectives  245 us (13%)
  other arithmetic  120 us (6%)
  local copies, waits for them, and re-layouts  84.7 us (4%)
    psum x1, waiting for transfers between devices, per_device(): lax.psum(jnp.einsum('tpc,tdc->pd', grad_pair_low, cross_pair, preferred_e...  204 us
    psum x1, waiting for transfers between devices, per_device(): lax.psum(summed[1].astype(jnp.bfloat16), 'rows').astype(jnp.float32)  116 us
    psum x1, waiting for transfers between devices, per_device(): lax.psum(jnp.dot(self_mixed, self_output, preferred_element_type=jnp.floa...  113 us
    psum x1, waiting for transfers between devices, per_device(): lax.psum(jnp.dot(cross_mixed, cross_output, preferred_element_type=jnp.fl...  85.7 us
    all_gather x8, blocking collectives, owner_key_grads(): lax.all_gather(row_total[:, :, 0].T, 'rows', axis=0, tiled=True)  76.4 us
    all_gather x8, blocking collectives, owner_key_grads(): lax.all_gather(spread[:, :, 0].T, 'rows', axis=0, tiled=True)  74.8 us
    dot_general x16, matrix products, scaled_scores(): jnp.einsum('qhe,khe->hqk', queries, key_rows, preferred_element_type=jnp....  70.2 us
    all_gather x8, waiting for transfers between devices, owner_key_grads(): lax.all_gather(queries, 'rows', axis=0, tiled=True)  69.2 us
  transfers between devices with their start and end apart: 38, of which 23 were waited for; matrix products, arithmetic and copies ran while one was open for 24% of the time, Pallas kernels for 0%

commit v1 on v0

--- a/solution.py
+++ b/solution.py
@@ -197,11 +197,14 @@
         cross_mixed, cross_peak, cross_total = attend_forward(
             by_heads(cross_queries), by_heads(cross_keys_all), by_heads(cross_values_all), mask_add
         )
-        cross_sum = lax.psum(
-            jnp.dot(cross_mixed, cross_output, preferred_element_type=jnp.float32).astype(
-                jnp.bfloat16
+        cross_sum = jnp.sum(
+            lax.all_gather(
+                jnp.dot(cross_mixed, cross_output, preferred_element_type=jnp.float32).astype(
+                    jnp.bfloat16
+                ),
+                "heads",
             ),
-            "heads",
+            axis=0,
         ).astype(jnp.float32)
         after_cross = after_self + cross_sum
         normed_three, norm_three_back = jax.vjp(gained, after_cross, hidden_gain_f)

time: 1920 us -> 2010 us (1.047)
  waiting for transfers between devices: 953 us -> 1030 us
    all_gather x0 -> x4, waiting for transfers between devices: none -> 155 us  [per_device(): lax.all_gather(jnp.dot(cross_mixed, cross_output, preferred_element_type=...]
    psum x1 -> x0, waiting for transfers between devices: 85.7 us -> none  [per_device(): lax.psum(jnp.dot(cross_mixed, cross_output, preferred_element_type=jnp.fl...]
    psum x1, waiting for transfers between devices: 113 us -> 134 us  [per_device(): lax.psum(jnp.dot(self_mixed, self_output, preferred_element_type=jnp.floa...]
    unnamed x673 -> x645, local copies, waits for them, and re-layouts: 42.7 us -> 49.1 us
  transfers between devices with their start and end apart: 38 -> 41, of which waited for: 23 -> 26; matrix products, arithmetic and copies ran while one was open for 24% -> 24% of each run, Pallas kernels for 0% -> 0%
where the time goes in v1:
time: 2010 us
  waiting for transfers between devices  1030 us (51%)
  matrix products  491 us (24%)
  blocking collectives  241 us (12%)
  other arithmetic  133 us (7%)
  local copies, waits for them, and re-layouts  91 us (5%)
    psum x1, waiting for transfers between devices, per_device(): lax.psum(jnp.einsum('tpc,tdc->pd', grad_pair_low, cross_pair, preferred_e...  204 us
    all_gather x4, waiting for transfers between devices, per_device(): lax.all_gather(jnp.dot(cross_mixed, cross_output, preferred_element_type=...  155 us
    psum x1, waiting for transfers between devices, per_device(): lax.psum(jnp.dot(self_mixed, self_output, preferred_element_type=jnp.floa...  134 us
    psum x1, waiting for transfers between devices, per_device(): lax.psum(summed[1].astype(jnp.bfloat16), 'rows').astype(jnp.float32)  116 us
    all_gather x8, blocking collectives, owner_key_grads(): lax.all_gather(spread[:, :, 0].T, 'rows', axis=0, tiled=True)  74.7 us
    all_gather x4, waiting for transfers between devices, per_device(): lax.all_gather(projected[2], 'rows', axis=0, tiled=True)  71.4 us
    all_gather x8, blocking collectives, owner_key_grads(): lax.all_gather(row_total[:, :, 0].T, 'rows', axis=0, tiled=True)  70.9 us
    all_gather x8, blocking collectives, owner_key_grads(): lax.all_gather(row_peak[:, :, 0].T, 'rows', axis=0, tiled=True)  70.3 us
  transfers between devices with their start and end apart: 41, of which 26 were waited for; matrix products, arithmetic and copies ran while one was open for 24% of the time, Pallas kernels for 0%

profile of v1, /device:TPU:0, one launch (start us, length us, event | category | flops | bytes accessed | tf_op | source)
XLA Modules:
  0.0 2005.3 jit_solution(10542483714751820575)
XLA Ops:
  34.8 11.2 all-gather.97.cloned.1.call-done
  53.5 18.0 all-gather.95.cloned.1.call-done
  77.1 19.9 all-gather.117.cloned.1.call-done
  104.5 17.8 all-gather.115.cloned.1.call-done
  128.0 20.3 %all-gather.107.cloned.1.call-done = bf16[1,2048,256]{1,2,0:T(8,128)(2,1)} async-done(((bf16[1,256,256]{1,2,0:T(8,128)(2,1)}), bf16[1,2048,256]{1,2,0:T(8,128)(2,1)}) %all-gather.107.cloned.1.call-update) | async-done | bytes 1048592 | tf_op jit(solution)/shard_map/all_gather | solution.py:169
  156.0 17.6 all-gather.105.cloned.1.call-done
  183.1 15.9 all-gather.87.cloned.1.call-done
  206.6 18.0 all-gather.85.cloned.1.call-done
  254.0 134.4 %all-reduce.20.cloned.1.call-done = (f32[256,1024]{1,0:T(8,128)}, f32[256,1024]{1,0:T(8,128)}, f32[256,1024]{1,0:T(8,128)}, f32[256,1024]{1,0:T(8,128)}) async-done(((f32[256,1024]{1,0:T(8,128)}, f32[256,1024]{1,0:T(8,128)}, f32[256,1024]{1,0:T(8,128)}, f32[256,1024]{1,0:T(8,128)}), (f32[256,1024]{1,0:T(8,128)}, f32[256,1024]{1,0:T(8,128)}, f32[256,1024]{1,0:T(8,128)}, ...) | async-done | bytes 4194320 | tf_op jit(solution)/shard_map/psum | solution.py:175
  404.8 10.0 all_gather.228
  414.8 9.9 all_gather.227
  424.8 8.2 all_gather.223
  432.9 9.9 all_gather.222
  442.9 8.1 all_gather.218
  451.0 9.0 all_gather.217
  460.0 8.1 all_gather.233
  468.1 9.0 all_gather.232
  523.7 17.8 all-gather.99.cloned.1.call-done
  549.2 17.8 all-gather.125.cloned.1.call-done
  573.0 19.5 all-gather.111.cloned.1.call-done
  600.2 17.8 all-gather.109.cloned.1.call-done
  625.0 18.6 all-gather.131.cloned.1.call-done
  649.6 19.4 all-gather.121.cloned.1.call-done
  676.8 9.0 all_gather.253
  694.0 9.0 all_gather.248
  711.1 9.4 all_gather.243
  728.6 9.0 all_gather.238
  777.9 19.6 all-gather.69.cloned.1.call-done
  803.8 41.8 %all-gather.93.cloned.1.call-done = bf16[1024,1024]{1,0:T(8,128)(2,1)} async-done(((bf16[256,1024]{1,0:T(8,128)(2,1)}), bf16[1024,1024]{1,0:T(8,128)(2,1)}) %all-gather.93.cloned.1.call-update) | async-done | bytes 2097168 | tf_op jit(solution)/shard_map/all_gather | solution.py:201
  848.5 43.8 %all-gather.103.cloned.1.call-done = bf16[1024,1024]{1,0:T(8,128)(2,1)} async-done(((bf16[256,1024]{1,0:T(8,128)(2,1)}), bf16[1024,1024]{1,0:T(8,128)(2,1)}) %all-gather.103.cloned.1.call-update) | async-done | bytes 2097168 | tf_op jit(solution)/shard_map/all_gather | solution.py:201
  899.2 40.1 %all-gather.113.cloned.1.call-done = bf16[1024,1024]{1,0:T(8,128)(2,1)} async-done(((bf16[256,1024]{1,0:T(8,128)(2,1)}), bf16[1024,1024]{1,0:T(8,128)(2,1)}) %all-gather.113.cloned.1.call-update) | async-done | bytes 2097168 | tf_op jit(solution)/shard_map/all_gather | solution.py:201
  956.6 29.6 %all-gather.123.cloned.1.call-done = bf16[1024,1024]{1,0:T(8,128)(2,1)} async-done(((bf16[256,1024]{1,0:T(8,128)(2,1)}), bf16[1024,1024]{1,0:T(8,128)(2,1)}) %all-gather.123.cloned.1.call-update) | async-done | bytes 2097168 | tf_op jit(solution)/shard_map/all_gather | solution.py:201
  1033.2 68.2 %all-reduce.28.cloned.1.call-done = (bf16[256,1024]{1,0:T(8,128)(2,1)}, bf16[256,1024]{1,0:T(8,128)(2,1)}, bf16[256,1024]{1,0:T(8,128)(2,1)}, bf16[256,1024]{1,0:T(8,128)(2,1)}) async-done(((bf16[256,1024]{1,0:T(8,128)(2,1)}, bf16[256,1024]{1,0:T(8,128)(2,1)}, bf16[256,1024]{1,0:T(8,128)(2,1)}, bf16[256,1024]{1,0:T(8,128)(2,1)}), (bf16[256,1024]{1,0:T(8,128)(2,1)}, bf16[256,1024]{1,0:T(8,128)(2,1)}, ...) | async-done | bytes 2097168 | tf_op jit(solution)/shard_map/psum | solution.py:234
  1134.6 9.0 all_gather.255
  1143.7 9.0 all_gather.250
  1169.4 8.1 all_gather.245
  1186.1 9.0 all_gather.240
  1272.0 61.3 %all-reduce.26.cloned.1.call-done = (bf16[256,1024]{1,0:T(8,128)(2,1)}, bf16[256,1024]{1,0:T(8,128)(2,1)}, bf16[256,1024]{1,0:T(8,128)(2,1)}, bf16[256,1024]{1,0:T(8,128)(2,1)}) async-done(((bf16[256,1024]{1,0:T(8,128)(2,1)}, bf16[256,1024]{1,0:T(8,128)(2,1)}, bf16[256,1024]{1,0:T(8,128)(2,1)}, bf16[256,1024]{1,0:T(8,128)(2,1)}), (bf16[256,1024]{1,0:T(8,128)(2,1)}, bf16[256,1024]{1,0:T(8,128)(2,1)}, ...) | async-done | bytes 2097168 | tf_op jit(solution)/shard_map/psum | solution.py:278
  1364.7 10.3 multiply_reduce_fusion.4
  1385.5 9.3 fusion.176
  1418.7 8.5 fusion.178
  1428.0 10.7 all_gather.230
  1438.7 9.3 all_gather.225
  1448.0 10.2 all_gather.220
  1458.2 9.3 all_gather.235
  1563.4 203.9 %all-reduce.24.cloned.1.call-done = (bf16[256,1024]{1,0:T(8,128)(2,1)}, bf16[256,1024]{1,0:T(8,128)(2,1)}, bf16[256,1024]{1,0:T(8,128)(2,1)}, bf16[256,1024]{1,0...) async-done(((bf16[256,1024]{1,0:T(8,128)(2,1)}, ...) | async-done | bytes 6291472 | tf_op jit(solution)/shard_map/psum | solution.py:284
  1814.7 24.8 %all-reduce.9 = (bf16[32,2,256]{2,1,0:T(2,128)(2,1)S(1)}, bf16[256]{0:T(256)(128)(2,1)S(1)}, bf16[256]{0:T(256)(128)(2,1)S(1)}) all-reduce(bf16[32,2,256]{2,1,0:T(2,128)(2,1)S(1)} %dynamic-slice_convert_fusion, bf16[256]{0:T(256)(128)(2,1)S(1)} %dynamic_slice.40, ...), channel_id=1, replica_groups=mesh['heads'=4,'rows'=8] {'rows'}, use_global_device_ids=true, to_apply=%region_100.101 | all-reduce | flops 16896 | bytes 67584 | tf_op jit(solution)/shard_map/psum | solution.py:364
  1861.6 116.2 %all-reduce.22.cloned.1.call-done = (bf16[3,1024,256]{1,2,0:T(8,128)(2,1)}, bf16[2,1024,256]{1,2,0:T(8,128)(2,1)}, bf16[768,256]{0,1:T(8,128)(2,1)}, bf16[256,10...) async-done(((bf16[3,1024,256]{1,2,0:T(8,128)(2,1)}, ...) | async-done | bytes 8781840 | tf_op jit(solution)/shard_map/psum | solution.py:365
  (1071 shorter events, 741.5 us)
Async XLA Ops:
  7.2 936.7 %copy-start = (bf16[1024,1024]{1,0:T(8,128)(2,1)S(1)}, bf16[1024,1024]{1,0:T(8,128)(2,1)}, u32[]{:S(2)}) copy-start(bf16[1024,1024]{1,0:T(8,128)(2,1)} %param.29) | copy-start | bytes 6291460
  7.2 38.8 %all-gather.97.cloned.1.call-start = ((), (), s32[]{:S(2)}) async-start(), calls=%async_computation.18 | async-start | bytes 1179648 | tf_op jit(solution)/shard_map/all_gather | solution.py:169
  19.6 51.9 %all-gather.95.cloned.1.call-start = ((), (), s32[]{:S(2)}) async-start(), calls=%async_computation.17 | async-start | bytes 1179648 | tf_op jit(solution)/shard_map/all_gather | solution.py:170
  20.4 76.6 %all-gather.117.cloned.1.call-start = ((), (), s32[]{:S(2)}) async-start(), calls=%async_computation.28 | async-start | bytes 1179648 | tf_op jit(solution)/shard_map/all_gather | solution.py:169
  23.3 99.0 %all-gather.115.cloned.1.call-start = ((), (), s32[]{:S(2)}) async-start(), calls=%async_computation.27 | async-start | bytes 1179648 | tf_op jit(solution)/shard_map/all_gather | solution.py:170
  23.9 124.4 %all-gather.107.cloned.1.call-start = ((), (), s32[]{:S(2)}) async-start(), calls=%async_computation.23 | async-start | bytes 1179648 | tf_op jit(solution)/shard_map/all_gather | solution.py:169
  26.8 146.7 %all-gather.105.cloned.1.call-start = ((), (), s32[]{:S(2)}) async-start(), calls=%async_computation.22 | async-start | bytes 1179648 | tf_op jit(solution)/shard_map/all_gather | solution.py:170
  27.4 171.6 %all-gather.87.cloned.1.call-start = ((), (), s32[]{:S(2)}) async-start(), calls=%async_computation.13 | async-start | bytes 1179648 | tf_op jit(solution)/shard_map/all_gather | solution.py:169
  33.8 190.7 %all-gather.85.cloned.1.call-start = ((), (), s32[]{:S(2)}) async-start(), calls=%async_computation.12 | async-start | bytes 1179648 | tf_op jit(solution)/shard_map/all_gather | solution.py:170
  34.6 353.7 %all-reduce.20.cloned.1.call-start = ((), (), s32[]{:S(2)}) async-start(), calls=%async_computation.36 | async-start | bytes 8388608 | tf_op jit(solution)/shard_map/psum | solution.py:175
  48.6 384.3 %copy-start.232 = (f32[4,256]{1,0:T(4,128)}, f32[4,256]{1,0:T(4,128)S(1)}, u32[]{:S(2)}) copy-start(f32[4,256]{1,0:T(4,128)S(1)} %get-tuple-element.215) | copy-start | bytes 12292
  53.4 371.3 %copy-start.257 = (f32[4,256]{1,0:T(4,128)}, f32[4,256]{1,0:T(4,128)S(1)}, u32[]{:S(2)}) copy-start(f32[4,256]{1,0:T(4,128)S(1)} %fusion.7) | copy-start | bytes 12292
  99.6 368.5 %copy-start.230 = (f32[4,256]{1,0:T(4,128)}, f32[4,256]{1,0:T(4,128)S(1)}, u32[]{:S(2)}) copy-start(f32[4,256]{1,0:T(4,128)S(1)} %get-tuple-element.211) | copy-start | bytes 12292
  104.5 355.5 %copy-start.255 = (f32[4,256]{1,0:T(4,128)}, f32[4,256]{1,0:T(4,128)S(1)}, u32[]{:S(2)}) copy-start(f32[4,256]{1,0:T(4,128)S(1)} %fusion.11) | copy-start | bytes 12292
  150.8 264.0 %copy-start.234 = (f32[4,256]{1,0:T(4,128)}, f32[4,256]{1,0:T(4,128)S(1)}, u32[]{:S(2)}) copy-start(f32[4,256]{1,0:T(4,128)S(1)} %get-tuple-element.209) | copy-start | bytes 12292
  201.7 249.3 %copy-start.235 = (f32[4,256]{1,0:T(4,128)}, f32[4,256]{1,0:T(4,128)S(1)}, u32[]{:S(2)}) copy-start(f32[4,256]{1,0:T(4,128)S(1)} %get-tuple-element.213) | copy-start | bytes 12292
  232.1 249.1 %all-gather.129.cloned.1.call-start = ((), (), s32[]{:S(2)}) async-start(), calls=%async_computation.34 | async-start | bytes 1179648 | tf_op jit(solution)/shard_map/all_gather | solution.py:93
  232.7 256.3 %all-gather.91.cloned.1.call-start = ((), (), s32[]{:S(2)}) async-start(), calls=%async_computation.15 | async-start | bytes 1179648 | tf_op jit(solution)/shard_map/all_gather | solution.py:193
  237.0 259.9 %all-gather.89.cloned.1.call-start = ((), (), s32[]{:S(2)}) async-start(), calls=%async_computation.14 | async-start | bytes 1179648 | tf_op jit(solution)/shard_map/all_gather | solution.py:194
  237.6 267.5 %all-gather.127.cloned.1.call-start = ((), (), s32[]{:S(2)}) async-start(), calls=%async_computation.33 | async-start | bytes 1179648 | tf_op jit(solution)/shard_map/all_gather | solution.py:93
  238.3 277.6 %all-gather.101.cloned.1.call-start = ((), (), s32[]{:S(2)}) async-start(), calls=%async_computation.20 | async-start | bytes 1179648 | tf_op jit(solution)/shard_map/all_gather | solution.py:193
  242.6 298.8 %all-gather.99.cloned.1.call-start = ((), (), s32[]{:S(2)}) async-start(), calls=%async_computation.19 | async-start | bytes 1179648 | tf_op jit(solution)/shard_map/all_gather | solution.py:194
  243.2 323.7 %all-gather.125.cloned.1.call-start = ((), (), s32[]{:S(2)}) async-start(), calls=%async_computation.32 | async-start | bytes 1179648 | tf_op jit(solution)/shard_map/all_gather | solution.py:93
  243.8 348.6 %all-gather.111.cloned.1.call-start = ((), (), s32[]{:S(2)}) async-start(), calls=%async_computation.25 | async-start | bytes 1179648 | tf_op jit(solution)/shard_map/all_gather | solution.py:193
  248.1 369.9 %all-gather.109.cloned.1.call-start = ((), (), s32[]{:S(2)}) async-start(), calls=%async_computation.24 | async-start | bytes 1179648 | tf_op jit(solution)/shard_map/all_gather | solution.py:194
  248.6 394.9 %all-gather.131.cloned.1.call-start = ((), (), s32[]{:S(2)}) async-start(), calls=%async_computation.35 | async-start | bytes 1179648 | tf_op jit(solution)/shard_map/all_gather | solution.py:93
  249.4 419.7 %all-gather.121.cloned.1.call-start = ((), (), s32[]{:S(2)}) async-start(), calls=%async_computation.30 | async-start | bytes 1179648 | tf_op jit(solution)/shard_map/all_gather | solution.py:193
  253.1 492.6 %all-gather.119.cloned.1.call-start = ((), (), s32[]{:S(2)}) async-start(), calls=%async_computation.29 | async-start | bytes 1179648 | tf_op jit(solution)/shard_map/all_gather | solution.py:194
  253.9 499.6 %all-gather.81.cloned.1.call-start = ((), (), s32[]{:S(2)}) async-start(), calls=%async_computation.10 | async-start | bytes 1179648 | tf_op jit(solution)/shard_map/all_gather | solution.py:93
  395.0 364.5 %all-gather.77.cloned.1.call-start = ((), (), s32[]{:S(2)}) async-start(), calls=%async_computation.8 | async-start | bytes 1179648 | tf_op jit(solution)/shard_map/all_gather | solution.py:93
  398.3 373.6 %all-gather.73.cloned.1.call-start = ((), (), s32[]{:S(2)}) async-start(), calls=%async_computation.6 | async-start | bytes 1179648 | tf_op jit(solution)/shard_map/all_gather | solution.py:93
  481.1 316.4 %all-gather.69.cloned.1.call-start = ((), (), s32[]{:S(2)}) async-start(), calls=%async_computation.4 | async-start | bytes 1179648 | tf_op jit(solution)/shard_map/all_gather | solution.py:93
  488.9 356.7 %all-gather.93.cloned.1.call-start = ((), (), s32[]{:S(2)}) async-start(), calls=%async_computation.16 | async-start | bytes 2621440 | tf_op jit(solution)/shard_map/all_gather | solution.py:201
  504.8 387.6 %all-gather.103.cloned.1.call-start = ((), (), s32[]{:S(2)}) async-start(), calls=%async_computation.21 | async-start | bytes 2621440 | tf_op jit(solution)/shard_map/all_gather | solution.py:201
  549.1 390.2 %all-gather.113.cloned.1.call-start = ((), (), s32[]{:S(2)}) async-start(), calls=%async_computation.26 | async-start | bytes 2621440 | tf_op jit(solution)/shard_map/all_gather | solution.py:201
  624.9 361.2 %all-gather.123.cloned.1.call-start = ((), (), s32[]{:S(2)}) async-start(), calls=%async_computation.31 | async-start | bytes 2621440 | tf_op jit(solution)/shard_map/all_gather | solution.py:201
  753.4 348.0 %all-reduce.28.cloned.1.call-start = ((), (), s32[]{:S(2)}) async-start(), calls=%async_computation.40 | async-start | bytes 4194304 | tf_op jit(solution)/shard_map/psum | solution.py:234
  1014.5 200.2 %all-gather.83.cloned.1.call-start = ((), (), s32[]{:S(2)}) async-start(), calls=%async_computation.11 | async-start | bytes 1179648 | tf_op jit(solution)/shard_map/all_gather | solution.py:94
  1127.4 98.2 %all-gather.79.cloned.1.call-start = ((), (), s32[]{:S(2)}) async-start(), calls=%async_computation.9 | async-start | bytes 1179648 | tf_op jit(solution)/shard_map/all_gather | solution.py:94
  1169.4 67.7 %all-gather.75.cloned.1.call-start = ((), (), s32[]{:S(2)}) async-start(), calls=%async_computation.7 | async-start | bytes 1179648 | tf_op jit(solution)/shard_map/all_gather | solution.py:94
  1186.1 63.0 %all-gather.71.cloned.1.call-start = ((), (), s32[]{:S(2)}) async-start(), calls=%async_computation.5 | async-start | bytes 1179648 | tf_op jit(solution)/shard_map/all_gather | solution.py:94
  1204.2 129.1 %all-reduce.26.cloned.1.call-start = ((), (), s32[]{:S(2)}) async-start(), calls=%async_computation.39 | async-start | bytes 4194304 | tf_op jit(solution)/shard_map/psum | solution.py:278
  1214.2 253.8 %all-gather.65.cloned.1.call-start = ((), (), s32[]{:S(2)}) async-start(), calls=%async_computation.2 | async-start | bytes 1179648 | tf_op jit(solution)/shard_map/all_gather | solution.py:94
  1350.6 133.0 %all-gather.63.cloned.1.call-start = ((), (), s32[]{:S(2)}) async-start(), calls=%async_computation.1 | async-start | bytes 1179648 | tf_op jit(solution)/shard_map/all_gather | solution.py:94
  1364.6 134.6 %all-gather.61.cloned.1.call-start = ((), (), s32[]{:S(2)}) async-start(), calls=%async_computation | async-start | bytes 1179648 | tf_op jit(solution)/shard_map/all_gather | solution.py:94
  1383.5 131.5 %all-gather.67.cloned.1.call-start = ((), (), s32[]{:S(2)}) async-start(), calls=%async_computation.3 | async-start | bytes 1179648 | tf_op jit(solution)/shard_map/all_gather | solution.py:94
  1467.5 299.8 %all-reduce.24.cloned.1.call-start = ((), (), s32[]{:S(2)}) async-start(), calls=%async_computation.38 | async-start | bytes 12582912 | tf_op jit(solution)/shard_map/psum | solution.py:284
  1541.5 436.3 %all-reduce.22.cloned.1.call-start = ((), (), s32[]{:S(2)}) async-start(), calls=%async_computation.37 | async-start | bytes 17563648 | tf_op jit(solution)/shard_map/psum | solution.py:365
  (314 other events, 7781.9 us)
Sparse Core Ops, SparseCore 0:
  19.7 26.2 all-gather.96
  47.9 23.5 all-gather.94
  73.4 23.5 all-gather.116
  98.7 23.5 all-gather.114
  124.6 23.5 all-gather.106
  150.0 23.5 all-gather.104
  175.4 23.5 all-gather.86
  200.9 23.5 all-gather.84
  232.3 156.0 all-reduce.19
  390.8 22.5 all-gather.128
  415.4 23.6 all-gather.90
  441.0 23.6 all-gather.88
  466.7 23.6 all-gather.126
  492.3 23.6 all-gather.100
  517.9 23.5 all-gather.98
  543.4 23.5 all-gather.124
  568.8 23.5 all-gather.110
  594.3 23.5 all-gather.108
  620.0 23.5 all-gather.130
  645.5 23.5 all-gather.120
  671.1 23.6 all-gather.118
  696.9 23.7 all-gather.80
  722.6 23.7 all-gather.76
  748.3 23.5 all-gather.72
  773.9 23.5 all-gather.68
  799.6 45.9 all-gather.92
  847.7 44.6 all-gather.102
  894.6 44.6 all-gather.112
  941.5 44.6 all-gather.122
  1014.6 86.7 all-reduce.27
  1127.5 22.6 all-gather.82
  1169.5 21.5 all-gather.78
  1192.9 23.6 all-gather.74
  1219.0 23.5 all-gather.70
  1245.2 88.0 all-reduce.25
  1350.8 22.4 all-gather.64
  1375.2 23.5 all-gather.62
  1401.4 23.6 all-gather.60
  1467.6 21.9 all-gather.66
  1541.6 225.6 all-reduce.23
  1847.4 130.3 all-reduce.21
